TPU v7x, 32 devices: a whole 2x2x4 slice. The times are simulated.
32 devices in a mesh: groups: 2 (over x), chan: 16 (over z, y, core).
Axes of the slice: x: 2, y: 2, z: 4, core: 2. Of those that a mesh axis runs over, the one named last changes fastest.
Arguments:
- data: bfloat16 [28672, 4096], P(('groups', 'chan')), parts along dimension 0, as said below
- alive: int32 [8192], P(('groups', 'chan')), parts along dimension 0, may hold values 0 or 1
- sources: int32 [2, 16], replicated, may hold values from 0 to 4095, as said below
Outputs:
- correlations: bfloat16 [4, 16, 256, 4096], P('groups', None, None, 'chan'), parts along dimension 0
There are 2 independent parts, one for each index of `groups`. A program takes and returns all parts, laid end to end along the dimension named above; an argument that names none is the same for every part. Nothing has to cross between parts.
Inputs may be any that keep to these rules, and one draw needn't show every extreme that they name: `sources`: no channel number appears twice in the array, and channel 4096 - 1 is always one of them. `data`: samples have channel and time-block scales of their own.
All inputs are finite; a program needn't handle non-finite values. No bound on the sum of `alive` on one device may be relied on, other than what follows from the above.
Results may differ from a plain program's by a relative error of at most 0.0076.
Values may be sent and summed in bfloat16 or wider, within the bound.
No kernel may reach another device: no remote copies, remote signals or barrier semaphores. Data moves between devices by JAX's collectives and lax.ppermute only.
A program may use at most 128 MiB of HBM per device.

v0:
```python
import math
import jax
import jax.numpy as jnp
from jax import lax
from jax.sharding import PartitionSpec as P

SEGMENT_LENGTH = 512
NF = 128
LAGS = 256
SRC = 16
ROUNDS = 2
SEGMENT_TALLY = 28


def forward_table():
    times = jnp.arange(SEGMENT_LENGTH, dtype=jnp.int32)[:, None]
    bins = jnp.arange(NF, dtype=jnp.int32)[None, :] + 1
    angle = 2.0 * math.pi / SEGMENT_LENGTH * (bins * times % SEGMENT_LENGTH).astype(jnp.float32)
    table = jnp.concatenate([jnp.cos(angle), -jnp.sin(angle)], axis=1) / math.sqrt(SEGMENT_LENGTH)
    return table.astype(jnp.bfloat16)


def inverse_table():
    shifts = jnp.arange(LAGS, dtype=jnp.int32)[:, None] - LAGS // 2
    bins = jnp.arange(NF, dtype=jnp.int32)[None, :] + 1
    angle = 2.0 * math.pi / SEGMENT_LENGTH * (bins * shifts % SEGMENT_LENGTH).astype(jnp.float32)
    return jnp.concatenate([jnp.cos(angle), -jnp.sin(angle)], axis=1).astype(jnp.bfloat16)


def body(data, alive, sources):
    count = lax.axis_size("chan")
    width = data.shape[1] // count
    table = forward_table()
    split = data.reshape(data.shape[0], count, width)
    moved = lax.all_to_all(split, "chan", split_axis=1, concat_axis=0, tiled=True)
    blocks = moved.reshape(SEGMENT_TALLY, SEGMENT_LENGTH, moved.shape[2])
    spectra = jnp.einsum("tk,wtc->wkc", table, blocks, preferred_element_type=jnp.float32)
    level = jnp.mean(spectra[:, :NF] ** 2 + spectra[:, NF:] ** 2, axis=0)
    factor = alive.astype(jnp.float32)[None, :] / jnp.sqrt(level + 0.01)
    factor = jnp.concatenate([factor, factor], axis=0)
    whitened = (spectra * factor[None]).astype(jnp.bfloat16)
    ids = sources.reshape(-1)
    owner = ids // width
    local = ids % width
    mine = owner == lax.axis_index("chan")
    picked = jnp.transpose(jnp.take(whitened, local, axis=2), (2, 0, 1)).astype(jnp.float32)
    picked = jnp.where(mine[:, None, None], picked, 0.0)
    src = lax.psum(picked, "chan").astype(jnp.bfloat16)
    src_re, src_im = (src[:, :, :NF], src[:, :, NF:])
    own_re, own_im = (whitened[:, :NF], whitened[:, NF:])
    form = "qwf,wfc->qfc"
    correlogram_realpart = jnp.einsum(
        form, src_re, own_re, preferred_element_type=jnp.float32
    ) + jnp.einsum(form, src_im, own_im, preferred_element_type=jnp.float32)
    cross_imaginary = jnp.einsum(
        form, src_re, own_im, preferred_element_type=jnp.float32
    ) - jnp.einsum(form, src_im, own_re, preferred_element_type=jnp.float32)
    cross = jnp.concatenate([correlogram_realpart, cross_imaginary], axis=1).astype(jnp.bfloat16)
    lagged = jnp.einsum("lk,qkc->qlc", inverse_table(), cross, preferred_element_type=jnp.float32)
    lagged = lagged / math.sqrt(NF * SEGMENT_TALLY)
    return lagged.reshape(ROUNDS, SRC, LAGS, width).astype(jnp.bfloat16)


def solution(mesh):
    return jax.shard_map(
        body,
        mesh=mesh,
        in_specs=(P(("groups", "chan"), None), P(("groups", "chan")), P()),
        out_specs=P("groups", None, None, "chan"),
        check_vma=False,
    )
```

profile of v0, /device:TPU:0, one launch (start us, length us, event | category | flops | bytes accessed | tf_op | source)
XLA Modules:
  0.0 326.9 jit_solution(7985542122648060904)
XLA Ops:
  0.0 6.9 %copy.27 = bf16[112,16,8,256]{3,2,0,1:T(8,128)(2,1)} copy(bf16[112,16,8,256]{3,2,1,0:T(8,128)(2,1)} %bitcast.32) | data formatting | bytes 14680064 | tf_op jit(solution)/shard_map/reshape | solution.py:34
  6.9 0.0 copy-start.3
  6.9 0.0 copy-start.2
  6.9 7.6 %all-to-all-start = ((bf16[896,16,256]{2,0,1:T(8,128)(2,1)}), bf16[896,16,256]{2,0,1:T(8,128)(2,1)}, u32[]{:S(2)}, u32[]{:S(2)}) async-start(bf16[896,16,256]{2,0,1:T(8,128)(2,1)} %bitcast.31), calls=%async_computation | async-start | bytes 14680064 | tf_op jit(solution)/shard_map/all_to_all | solution.py:35
  14.4 0.0 copy-done.3
  14.4 0.1 reshape.125
  14.5 0.1 reshape.124
  14.6 0.0 copy-done.2
  14.7 0.6 cosine_convert_fusion
  15.3 1.1 fusion.33
  16.4 130.5 %all-to-all-done = bf16[896,16,256]{2,0,1:T(8,128)(2,1)} async-done(((bf16[896,16,256]{2,0,1:T(8,128)(2,1)}), bf16[896,16,256]{2,0,1:T(8,128)(2,1)}, u32[]{:S(2)}, u32[]{:S(2)}) %all-to-all-start) | async-done | bytes 7340064 | tf_op jit(solution)/shard_map/all_to_all | solution.py:35
  146.9 5.2 %convolution_bitcast_fusion = f32[28,256,256]{2,1,0:T(8,128)S(1)} fusion(bf16[28,512,256]{2,1,0:T(8,128)(2,1)} %bitcast.3, f32[512,128]{0,1:T(8,128)S(1)} %get-tuple-element.14, f32[512,128]{0,1:T(8,128)S(1)} %get-tuple-element.13), kind=kOutput, calls=%fused_computation.14 | convolution fusion | flops 1879441408 | bytes 15204352 | tf_op jit(solution)/shard_map/tk,wtc->wkc/dot_general | solution.py:37
  152.0 0.5 fusion.5
  152.6 2.6 multiply_convert_fusion.1
  155.2 7.7 %copy.7 = bf16[28,256,256]{1,0,2:T(8,128)(2,1)} copy(bf16[28,256,256]{2,1,0:T(8,128)(2,1)} %multiply_convert_fusion.1) | data formatting | bytes 7340032 | tf_op jit(solution)/shard_map/convert_element_type | solution.py:41
  162.9 3.6 %fusion.40 = (bf16[28,128,256]{2,1,0:T(8,128)(2,1)S(1)}, bf16[28,128,256]{2,1,0:T(8,128)(2,1)}) fusion(bf16[28,256,256]{2,1,0:T(8,128)(2,1)} %multiply_convert_fusion.1), kind=kLoop, calls=%fused_computation.76 | loop fusion | bytes 7340032 | tf_op jit(solution)/shard_map/slice | solution.py:50
  166.6 2.8 gather_fusion
  169.3 0.2 convert_select_fusion
  169.6 100.6 %all-reduce.1 = bf16[32,28,256]{2,1,0:T(8,128)(2,1)S(1)} all-reduce(f32[32,28,256]{2,1,0:T(8,128)S(1)} %convert_select_fusion), channel_id=1, replica_groups=mesh['groups'=2,'chan'=16] {'chan'}, use_global_device_ids=true, to_apply=%region_1.2 | all-reduce | flops 229376 | bytes 1376256 | tf_op jit(solution)/shard_map/psum | solution.py:48
  270.2 0.1 fusion.41
  270.3 2.6 copy.13
  272.8 1.6 copy.10
  274.5 0.0 copy-start
  274.5 0.0 copy-start.1
  274.5 4.6 %fusion.14 = f32[128,256,32]{1,2,0:T(8,128)} fusion(bf16[32,28,128]{0,1,2:T(8,128)(2,1)} %copy.13, bf16[28,128,256]{2,1,0:T(8,128)(2,1)S(1)} %get-tuple-element.5), kind=kOutput, calls=%fused_computation.21 | convolution fusion | flops 58720256 | bytes 6258688 | tf_op jit(solution)/shard_map/qwf,wfc->qfc/dot_general | solution.py:57
  279.1 0.0 copy-done
  279.1 0.0 copy-done.1
  279.1 3.2 fusion.12
  282.4 3.3 fusion.10
  285.6 3.3 %fusion.16 = f32[128,256,32]{1,2,0:T(8,128)} fusion(bf16[32,28,128]{0,1,2:T(8,128)(2,1)S(1)} %copy.10, bf16[28,128,256]{2,1,0:T(8,128)(2,1)S(1)} %get-tuple-element.5), kind=kOutput, calls=%fused_computation.23 | convolution fusion | flops 58720256 | bytes 6258688 | tf_op jit(solution)/shard_map/qwf,wfc->qfc/dot_general | solution.py:52
  288.9 5.3 %copy.16 = f32[128,256,32]{0,1,2:T(8,128)} copy(f32[128,256,32]{1,2,0:T(8,128)} %fusion.14) | data formatting | bytes 8388608 | tf_op jit(solution)/shard_map/qwf,wfc->qfc/dot_general | solution.py:57
  294.2 5.3 %copy.15 = f32[128,256,32]{0,1,2:T(8,128)} copy(f32[128,256,32]{1,2,0:T(8,128)} %fusion.10) | data formatting | bytes 8388608 | tf_op jit(solution)/shard_map/qwf,wfc->qfc/dot_general | solution.py:55
  299.6 5.3 %copy.14 = f32[128,256,32]{0,1,2:T(8,128)} copy(f32[128,256,32]{1,2,0:T(8,128)} %fusion.12) | data formatting | bytes 8388608 | tf_op jit(solution)/shard_map/qwf,wfc->qfc/dot_general | solution.py:54
  304.9 5.3 %copy.11 = f32[128,256,32]{0,1,2:T(8,128)} copy(f32[128,256,32]{1,2,0:T(8,128)} %fusion.16) | data formatting | bytes 8388608 | tf_op jit(solution)/shard_map/qwf,wfc->qfc/dot_general | solution.py:52
  310.2 7.6 %fusion.8 = (bf16[32,128,256]{1,2,0:T(8,128)(2,1)S(1)}, bf16[32,128,256]{1,2,0:T(8,128)(2,1)S(1)}) fusion(f32[128,256,32]{0,1,2:T(8,128)} %copy.11, f32[128,256,32]{0,1,2:T(8,128)} %copy.14, f32[128,256,32]{0,1,2:T(8,128)} %copy.15, f32[128,256,32]{0,1,2:T(8,128)} %copy.16), kind=kLoop, calls=%fused_computation.15 | loop fusion | flops 4194304 | bytes 20971520 | tf_op jit(solution)/shard_map/add | solution.py:52
  317.8 2.9 multiply_convert_fusion
  320.7 6.2 %copy.8 = bf16[2,16,256,256]{3,2,1,0:T(8,128)(2,1)} copy(bf16[2,16,256,256]{2,3,1,0:T(8,128)(2,1)} %bitcast.33) | data formatting | bytes 8388608 | tf_op jit(solution)/shard_map/convert_element_type | solution.py:61
  (8 shorter events, 0.1 us)
Async XLA Ops:
  6.9 7.6 %copy-start.3 = (s32[2,16]{1,0:T(2,128)S(1)}, s32[2,16]{1,0:T(2,128)}, u32[]{:S(2)}) copy-start(s32[2,16]{1,0:T(2,128)} %param.5) | copy-start | bytes 388
  6.9 7.8 %copy-start.2 = (s32[256]{0:T(256)S(1)}, s32[256]{0:T(256)}, u32[]{:S(2)}) copy-start(s32[256]{0:T(256)} %param.4) | copy-start | bytes 3076
  6.9 140.0 %all-to-all-start = ((bf16[896,16,256]{2,0,1:T(8,128)(2,1)}), bf16[896,16,256]{2,0,1:T(8,128)(2,1)}, u32[]{:S(2)}, u32[]{:S(2)}) async-start(bf16[896,16,256]{2,0,1:T(8,128)(2,1)} %bitcast.31), calls=%async_computation | async-start | bytes 14680064 | tf_op jit(solution)/shard_map/all_to_all | solution.py:35
  274.5 4.7 %copy-start = (bf16[28,128,256]{2,1,0:T(8,128)(2,1)S(1)}, bf16[28,128,256]{2,1,0:T(8,128)(2,1)}, u32[]{:S(2)}) copy-start(bf16[28,128,256]{2,1,0:T(8,128)(2,1)} %get-tuple-element.6) | copy-start | bytes 5505028
  274.5 4.7 %copy-start.1 = (bf16[32,28,128]{0,1,2:T(8,128)(2,1)S(1)}, bf16[32,28,128]{0,1,2:T(8,128)(2,1)}, u32[]{:S(2)}) copy-start(bf16[32,28,128]{0,1,2:T(8,128)(2,1)} %copy.13) | copy-start | bytes 688132
where the time goes:
time: 328 us; the launch traced here: 327 us
  waiting for transfers between devices  130 us (40%)
  blocking collectives  101 us (31%)
  local copies, waits for them, and re-layouts  52.9 us (16%)
  matrix products  22.5 us (7%)
  other arithmetic  12.8 us (4%)
  starting transfers between devices  7.56 us (2%)
    all_to_all x1, waiting for transfers between devices, body(): lax.all_to_all(split, 'chan', split_axis=1, concat_axis=0, tiled=True)  130 us
    psum x1, blocking collectives, body(): src = lax.psum(picked, 'chan').astype(jnp.bfloat16)  101 us
    convert_element_type x1, local copies, waits for them, and re-layouts, body(): whitened = (spectra * factor[None]).astype(jnp.bfloat16)  7.7 us
    add x1, other arithmetic, body(): jnp.einsum(form, src_re, own_re, preferred_element_type=jnp.float32)  7.63 us
    all_to_all x1, starting transfers between devices, body(): lax.all_to_all(split, 'chan', split_axis=1, concat_axis=0, tiled=True)  7.56 us
    reshape x1, local copies, waits for them, and re-layouts, body(): split = data.reshape(data.shape[0], count, width)  6.85 us
  transfers between devices with their start and end apart: 1, of which 1 were waited for; matrix products, arithmetic and copies ran while one was open for 1% of the time, Pallas kernels for 0%

commit v1 on v0

--- a/solution.py
+++ b/solution.py
@@ -10,6 +10,29 @@
 SRC = 16
 ROUNDS = 2
 SEGMENT_TALLY = 28
+
+
+def split_up(shard, dim, peers):
+    before, after = (shard.shape[:dim], shard.shape[dim + 1 :])
+    return jnp.moveaxis(shard.reshape(*before, peers, -1, *after), dim, 0)
+
+
+def joined_along(parts, dim):
+    parts = jnp.moveaxis(parts, 0, dim)
+    lengths = parts.shape
+    return parts.reshape(*lengths[:dim], lengths[dim] * lengths[dim + 1], *lengths[dim + 2 :])
+
+
+def rotated_exchange(x, axis, split_dim, concat_dim):
+    count, index = (lax.axis_size(axis), lax.axis_index(axis))
+    tiles = split_up(x, split_dim, count)
+    out = tiles
+    for step in range(1, count):
+        target, source = ((index + step) % count, (index - step) % count)
+        sent = lax.dynamic_index_in_dim(tiles, target, 0)
+        other = lax.ppermute(sent, axis, [(i, (i + step) % count) for i in range(count)])
+        out = lax.dynamic_update_slice_in_dim(out, other, source, axis=0)
+    return joined_along(out, concat_dim)
 
 
 def forward_table():
@@ -32,7 +55,7 @@
     width = data.shape[1] // count
     table = forward_table()
     split = data.reshape(data.shape[0], count, width)
-    moved = lax.all_to_all(split, "chan", split_axis=1, concat_axis=0, tiled=True)
+    moved = rotated_exchange(split, "chan", 1, 0)
     blocks = moved.reshape(SEGMENT_TALLY, SEGMENT_LENGTH, moved.shape[2])
     spectra = jnp.einsum("tk,wtc->wkc", table, blocks, preferred_element_type=jnp.float32)
     level = jnp.mean(spectra[:, :NF] ** 2 + spectra[:, NF:] ** 2, axis=0)

time: 328 us -> 351 us (1.070)
  starting transfers between devices: 7.56 us -> 81.6 us
  waiting for transfers between devices: 130 us -> 76.4 us
  local copies, waits for them, and re-layouts: 52.9 us -> 69.4 us
  other arithmetic: 12.8 us -> 6.3 us
  matrix products: 22.5 us -> 16.9 us
  blocking collectives: 101 us -> 96.2 us
    all_to_all x1 -> x0, waiting for transfers between devices: 130 us -> none  [body(): lax.all_to_all(split, 'chan', split_axis=1, concat_axis=0, tiled=True)]
    ppermute x0 -> x15, starting transfers between devices: none -> 81.6 us  [rotated_exchange(): lax.ppermute(sent, axis, [(i, (i + step) % count) for i in range(count)])]
    ppermute x0 -> x15, waiting for transfers between devices: none -> 76.4 us  [rotated_exchange(): lax.ppermute(sent, axis, [(i, (i + step) % count) for i in range(count)])]
    dynamic_update_slice x0 -> x16, local copies, waits for them, and re-layouts: none -> 23.4 us  [rotated_exchange(): out = lax.dynamic_update_slice_in_dim(out, other, source, axis=0)]
    dot_general x4 -> x0, local copies, waits for them, and re-layouts: 21.3 us -> none  [the longest x1 5.34 us: body(): jnp.einsum(form, src_re, own_im, preferred_element_type=jnp.float32)]
    unnamed x8 -> x17, local copies, waits for them, and re-layouts: 0.02 us -> 11.7 us
    slice x1 -> x3, local copies, waits for them, and re-layouts: 3.64 us -> 11.8 us  [body(): own_re, own_im = (whitened[:, :NF], whitened[:, NF:])]
    add x1 -> x0, other arithmetic: 7.63 us -> none  [body(): jnp.einsum(form, src_re, own_re, preferred_element_type=jnp.float32)]
  transfers between devices with their start and end apart: 1 -> 15, of which waited for: 1 -> 5; matrix products, arithmetic and copies ran while one was open for 1% -> 4% of each run, Pallas kernels for 0% -> 0%
where the time goes in v1:
time: 351 us; the launch traced here: 347 us
  blocking collectives  96.2 us (27%)
  starting transfers between devices  81.6 us (23%)
  waiting for transfers between devices  76.4 us (22%)
  local copies, waits for them, and re-layouts  69.4 us (20%)
  matrix products  16.9 us (5%)
  other arithmetic  6.3 us (2%)
    psum x1, blocking collectives, body(): src = lax.psum(picked, 'chan').astype(jnp.bfloat16)  96.2 us
    ppermute x15, starting transfers between devices, rotated_exchange(): lax.ppermute(sent, axis, [(i, (i + step) % count) for i in range(count)])  81.6 us
    ppermute x15, waiting for transfers between devices, rotated_exchange(): lax.ppermute(sent, axis, [(i, (i + step) % count) for i in range(count)])  76.4 us
    dynamic_update_slice x16, local copies, waits for them, and re-layouts, rotated_exchange(): out = lax.dynamic_update_slice_in_dim(out, other, source, axis=0)  23.4 us
    slice x3, local copies, waits for them, and re-layouts, body(): own_re, own_im = (whitened[:, :NF], whitened[:, NF:])  11.8 us
    unnamed x17, local copies, waits for them, and re-layouts  11.7 us
    dot_general x1, matrix products, body(): jnp.einsum('lk,qkc->qlc', inverse_table(), cross, preferred_element_type=...  7.24 us
  transfers between devices with their start and end apart: 15, of which 5 were waited for; matrix products, arithmetic and copies ran while one was open for 4% of the time, Pallas kernels for 0%

profile of v1, /device:TPU:0, one launch (start us, length us, event | category | flops | bytes accessed | tf_op | source)
XLA Modules:
  0.0 347.4 jit_solution(12167967714740710702)
XLA Ops:
  0.0 10.8 %copy.8 = bf16[896,4096]{0,1:T(8,128)(2,1)} copy(bf16[896,4096]{1,0:T(8,128)(2,1)} %param.3) | data formatting | bytes 14680064 | tf_op args[0]
  10.8 5.7 %dynamic-slice_bitcast_fusion = (bf16[1,896,1,256]{1,3,0,2:T(8,128)(2,1)S(1)}, bf16[1,896,1,256]{1,3,0,2:T(8,128)(2,1)}, bf16[1,896,1,256]{1,3,0,2:T(8,128)(2,1)...) fusion(bf16[896,16,1,256]{0,3,1,2:T(8,128)(2,1)} %bitcast.56, ...), kind=kLoop, calls=%fused_computation.24 | loop fusion | bytes 13762620 | tf_op jit(solution)/shard_map/jit(dynamic_index_in_dim)/dynamic_slice | solution.py:32
  17.0 2.6 collective-permute-start.1
  19.6 2.4 collective-permute-start.2
  22.0 1.6 collective-permute-start.3
  23.8 1.1 fusion.29
  26.0 6.4 %collective-permute-done = bf16[1,896,1,256]{1,3,0,2:T(8,128)(2,1)S(1)} collective-permute-done((bf16[1,896,1,256]{1,3,0,2:T(8,128)(2,1)}, bf16[1,896,1,256]{1,3,0,2:T(8,128)(2,1)S(1)}, u32[]{:S(2)}, u32[]{:S(2)}) %collective-permute-start) | collective-permute-done | bytes 458784 | tf_op jit(solution)/shard_map/ppermute | solution.py:33
  33.0 0.8 constant_dynamic-update-slice_fusion.14
  34.3 9.2 %collective-permute-start.6 = (bf16[1,896,1,256]{1,3,0,2:T(8,128)(2,1)}, bf16[1,896,1,256]{1,3,0,2:T(8,128)(2,1)S(1)}, u32[]{:S(2)}, u32[]{:S(2)}) collective-permute-start(bf16[1,896,1,256]{1,3,0,2:T(8,128)(2,1)} %get-tuple-element.13), channel_id=1, source_target_pairs={{0,7},{1,8},{2,9},{3,10},{4,11},{5,12},{6,13},{7,14},{8,15},{9,0},... | collective-permute-start | bytes 1376264 | tf_op jit(solution)/shard_map/ppermute | solution.py:33
  43.5 0.8 constant_dynamic-update-slice_fusion.13
  44.3 1.7 collective-permute-start.7
  45.9 0.8 constant_dynamic-update-slice_fusion.12
  47.0 0.8 constant_dynamic-update-slice_fusion.11
  47.8 64.0 %collective-permute-done.4 = bf16[1,896,1,256]{1,3,0,2:T(8,128)(2,1)S(1)} collective-permute-done((bf16[1,896,1,256]{1,3,0,2:T(8,128)(2,1)}, bf16[1,896,1,256]{1,3,0,2:T(8,128)(2,1)S(1)}, u32[]{:S(2)}, u32[]{:S(2)}) %collective-permute-start.4) | collective-permute-done | bytes 458784 | tf_op jit(solution)/shard_map/ppermute | solution.py:33
  111.8 0.8 constant_dynamic-update-slice_fusion.10
  112.7 11.4 %collective-permute-start.10 = (bf16[1,896,1,256]{1,3,0,2:T(8,128)(2,1)S(1)}, bf16[1,896,1,256]{1,3,0,2:T(8,128)(2,1)S(1)}, u32[]{:S(2)}, u32[]{:S(2)}) collective-permute-start(bf16[1,896,1,256]{1,3,0,2:T(8,128)(2,1)S(1)} %copy-done.5), channel_id=1, source_target_pairs={{0,11},{1,12},{2,13},{3,14},{4,15},{5,0},{6,1},{7,2},{8,3},{9,4},{... | collective-permute-start | bytes 1376264 | tf_op jit(solution)/shard_map/ppermute | solution.py:33
  124.1 0.8 constant_dynamic-update-slice_fusion.9
  124.9 23.1 %collective-permute-start.11 = (bf16[1,896,1,256]{1,3,0,2:T(8,128)(2,1)S(1)}, bf16[1,896,1,256]{1,3,0,2:T(8,128)(2,1)S(1)}, u32[]{:S(2)}, u32[]{:S(2)}) collective-permute-start(bf16[1,896,1,256]{1,3,0,2:T(8,128)(2,1)S(1)} %copy-done.4), channel_id=1, source_target_pairs={{0,12},{1,13},{2,14},{3,15},{4,0},{5,1},{6,2},{7,3},{8,4},{9,5},{1... | collective-permute-start | bytes 1376264 | tf_op jit(solution)/shard_map/ppermute | solution.py:33
  148.1 0.8 constant_dynamic-update-slice_fusion.8
  149.3 0.8 constant_dynamic-update-slice_fusion.7
  150.1 14.5 %collective-permute-start.13 = (bf16[1,896,1,256]{1,3,0,2:T(8,128)(2,1)S(1)}, bf16[1,896,1,256]{1,3,0,2:T(8,128)(2,1)S(1)}, u32[]{:S(2)}, u32[]{:S(2)}) collective-permute-start(bf16[1,896,1,256]{1,3,0,2:T(8,128)(2,1)S(1)} %copy-done.2), channel_id=1, source_target_pairs={{0,14},{1,15},{2,0},{3,1},{4,2},{5,3},{6,4},{7,5},{8,6},{9,7},{10,... | collective-permute-start | bytes 1376264 | tf_op jit(solution)/shard_map/ppermute | solution.py:33
  164.6 0.8 constant_dynamic-update-slice_fusion.6
  165.4 13.3 %collective-permute-start.14 = (bf16[1,896,1,256]{1,3,0,2:T(8,128)(2,1)S(1)}, bf16[1,896,1,256]{1,3,0,2:T(8,128)(2,1)S(1)}, u32[]{:S(2)}, u32[]{:S(2)}) collective-permute-start(bf16[1,896,1,256]{1,3,0,2:T(8,128)(2,1)S(1)} %get-tuple-element.5), channel_id=1, source_target_pairs={{0,15},{1,0},{2,1},{3,2},{4,3},{5,4},{6,5},{7,6},{8,7},{9,8},{10,9... | collective-permute-start | bytes 1376264 | tf_op jit(solution)/shard_map/ppermute | solution.py:33
  178.7 0.8 constant_dynamic-update-slice_fusion.5
  179.5 0.8 constant_dynamic-update-slice_fusion.4
  180.4 0.8 constant_dynamic-update-slice_fusion.3
  181.2 0.8 constant_dynamic-update-slice_fusion.2
  182.0 2.9 collective-permute-done.13
  184.9 0.8 constant_dynamic-update-slice_fusion.1
  185.8 2.5 collective-permute-done.14
  188.2 0.8 constant_dynamic-update-slice_fusion
  189.1 11.2 %copy.9 = bf16[16,896,1,256]{3,1,0,2:T(8,128)(2,1)} copy(bf16[16,896,1,256]{1,3,0,2:T(8,128)(2,1)} %constant_dynamic-update-slice_fusion) | data formatting | bytes 14680064 | tf_op jit(solution)/shard_map/dynamic_update_slice | solution.py:34
  200.3 5.2 %convolution_bitcast_fusion = f32[28,256,256]{1,2,0:T(8,128)S(1)} fusion(bf16[28,512,256]{2,1,0:T(8,128)(2,1)} %bitcast.58, f32[512,128]{1,0:T(8,128)S(1)} %get-tuple-element.27, f32[512,128]{1,0:T(8,128)S(1)} %get-tuple-element.26), kind=kOutput, calls=%fused_computation.13 | convolution fusion | flops 1879441408 | bytes 15204352 | tf_op jit(solution)/shard_map/tk,wtc->wkc/dot_general | solution.py:60
  206.1 1.0 multiply_convert_fusion.1
  207.1 4.2 %copy.11 = bf16[28,256,256]{1,0,2:T(8,128)(2,1)} copy(bf16[28,256,256]{1,2,0:T(8,128)(2,1)S(1)} %multiply_convert_fusion.1) | data formatting | bytes 7340032 | tf_op jit(solution)/shard_map/convert_element_type | solution.py:64
  211.3 2.9 fusion.36
  214.2 2.8 gather_fusion
  216.9 3.4 copy.12
  220.4 2.7 convert_select_fusion
  223.1 96.2 %all-reduce.1 = bf16[32,28,256]{1,0,2:T(8,128)(2,1)S(1)} all-reduce(f32[32,28,256]{1,0,2:T(8,128)} %convert_select_fusion), channel_id=1, replica_groups=mesh['groups'=2,'chan'=16] {'chan'}, use_global_device_ids=true, to_apply=%region_1.2 | all-reduce | flops 229376 | bytes 1376256 | tf_op jit(solution)/shard_map/psum | solution.py:71
  319.2 4.5 %copy.13 = bf16[28,128,256]{2,0,1:T(8,128)(2,1)} copy(bf16[28,128,256]{1,2,0:T(8,128)(2,1)} %get-tuple-element.20) | data formatting | bytes 3670016 | tf_op jit(solution)/shard_map/slice | solution.py:73
  323.8 4.4 %copy.14 = bf16[28,128,256]{2,0,1:T(8,128)(2,1)} copy(bf16[28,128,256]{1,2,0:T(8,128)(2,1)} %get-tuple-element.21) | data formatting | bytes 3670016 | tf_op jit(solution)/shard_map/slice | solution.py:73
  328.2 2.4 fusion.12
  331.3 0.7 fusion.6
  332.0 0.9 copy-done
  332.9 0.7 fusion.7
  334.0 7.2 %multiply_convert_fusion = bf16[32,256,256]{2,1,0:T(8,128)(2,1)} fusion(bf16[32,256,256]{2,0,1:T(8,128)(2,1)S(1)} %pad_maximum_fusion, bf16[256,128]{1,0:T(8,128)(2,1)S(1)} %get-tuple-element.23, bf16[256,128]{1,0:T(8,128)(2,1)S(1)} %get-tuple-element.22), kind=kOutput, calls=%fused_computation.1 | convolution fusion | flops 1078198272 | bytes 8519680 | tf_op jit(solution)/shard_map/lk,qkc->qlc/dot_general | solution.py:82
  341.2 6.2 %copy.18 = bf16[2,16,256,256]{3,2,1,0:T(8,128)(2,1)} copy(bf16[2,16,256,256]{2,3,1,0:T(8,128)(2,1)} %bitcast.59) | data formatting | bytes 8388608 | tf_op jit(solution)/shard_map/convert_element_type | solution.py:84
  (46 shorter events, 4.9 us)
Async XLA Ops:
  10.8 14.0 %copy-start.7 = (s32[2,16]{1,0:T(2,128)S(1)}, s32[2,16]{1,0:T(2,128)}, u32[]{:S(2)}) copy-start(s32[2,16]{1,0:T(2,128)} %param.5) | copy-start | bytes 388
  10.8 15.1 %copy-start.6 = (s32[256]{0:T(256)S(1)}, s32[256]{0:T(256)}, u32[]{:S(2)}) copy-start(s32[256]{0:T(256)} %param.4) | copy-start | bytes 3076
  16.5 16.0 %collective-permute-start = (bf16[1,896,1,256]{1,3,0,2:T(8,128)(2,1)}, bf16[1,896,1,256]{1,3,0,2:T(8,128)(2,1)S(1)}, u32[]{:S(2)}, u32[]{:S(2)}) collective-permute-start(bf16[1,896,1,256]{1,3,0,2:T(8,128)(2,1)} %get-tuple-element.19), channel_id=1, source_target_pairs={{0,1},{1,2},{2,3},{3,4},{4,5},{5,6},{6,7},{7,8},{8,9},{9,10},{10,1... | collective-permute-start | bytes 1376264 | tf_op jit(solution)/shard_map/ppermute | solution.py:33
  17.0 17.3 %collective-permute-start.1 = (bf16[1,896,1,256]{1,3,0,2:T(8,128)(2,1)}, bf16[1,896,1,256]{1,3,0,2:T(8,128)(2,1)S(1)}, u32[]{:S(2)}, u32[]{:S(2)}) collective-permute-start(bf16[1,896,1,256]{1,3,0,2:T(8,128)(2,1)} %get-tuple-element.18), channel_id=1, source_target_pairs={{0,2},{1,3},{2,4},{3,5},{4,6},{5,7},{6,8},{7,9},{8,10},{9,11},{10,... | collective-permute-start | bytes 1376264 | tf_op jit(solution)/shard_map/ppermute | solution.py:33
  19.6 24.7 %collective-permute-start.2 = (bf16[1,896,1,256]{1,3,0,2:T(8,128)(2,1)}, bf16[1,896,1,256]{1,3,0,2:T(8,128)(2,1)S(1)}, u32[]{:S(2)}, u32[]{:S(2)}) collective-permute-start(bf16[1,896,1,256]{1,3,0,2:T(8,128)(2,1)} %get-tuple-element.17), channel_id=1, source_target_pairs={{0,3},{1,4},{2,5},{3,6},{4,7},{5,8},{6,9},{7,10},{8,11},{9,12},{10... | collective-permute-start | bytes 1376264 | tf_op jit(solution)/shard_map/ppermute | solution.py:33
  22.0 24.8 %collective-permute-start.3 = (bf16[1,896,1,256]{1,3,0,2:T(8,128)(2,1)}, bf16[1,896,1,256]{1,3,0,2:T(8,128)(2,1)S(1)}, u32[]{:S(2)}, u32[]{:S(2)}) collective-permute-start(bf16[1,896,1,256]{1,3,0,2:T(8,128)(2,1)} %get-tuple-element.16), channel_id=1, source_target_pairs={{0,4},{1,5},{2,6},{3,7},{4,8},{5,9},{6,10},{7,11},{8,12},{9,13},{1... | collective-permute-start | bytes 1376264 | tf_op jit(solution)/shard_map/ppermute | solution.py:33
  23.6 88.3 %collective-permute-start.4 = (bf16[1,896,1,256]{1,3,0,2:T(8,128)(2,1)}, bf16[1,896,1,256]{1,3,0,2:T(8,128)(2,1)S(1)}, u32[]{:S(2)}, u32[]{:S(2)}) collective-permute-start(bf16[1,896,1,256]{1,3,0,2:T(8,128)(2,1)} %get-tuple-element.15), channel_id=1, source_target_pairs={{0,5},{1,6},{2,7},{3,8},{4,9},{5,10},{6,11},{7,12},{8,13},{9,14},{... | collective-permute-start | bytes 1376264 | tf_op jit(solution)/shard_map/ppermute | solution.py:33
  26.0 86.7 %copy-start.5 = (bf16[1,896,1,256]{1,3,0,2:T(8,128)(2,1)S(1)}, bf16[1,896,1,256]{1,3,0,2:T(8,128)(2,1)}, u32[]{:S(2)}) copy-start(bf16[1,896,1,256]{1,3,0,2:T(8,128)(2,1)} %get-tuple-element.9) | copy-start | bytes 1376260
  26.0 98.9 %copy-start.4 = (bf16[1,896,1,256]{1,3,0,2:T(8,128)(2,1)S(1)}, bf16[1,896,1,256]{1,3,0,2:T(8,128)(2,1)}, u32[]{:S(2)}) copy-start(bf16[1,896,1,256]{1,3,0,2:T(8,128)(2,1)} %get-tuple-element.8) | copy-start | bytes 1376260
  26.0 122.9 %copy-start.3 = (bf16[1,896,1,256]{1,3,0,2:T(8,128)(2,1)S(1)}, bf16[1,896,1,256]{1,3,0,2:T(8,128)(2,1)}, u32[]{:S(2)}) copy-start(bf16[1,896,1,256]{1,3,0,2:T(8,128)(2,1)} %get-tuple-element.7) | copy-start | bytes 1376260
  26.0 124.1 %copy-start.2 = (bf16[1,896,1,256]{1,3,0,2:T(8,128)(2,1)S(1)}, bf16[1,896,1,256]{1,3,0,2:T(8,128)(2,1)}, u32[]{:S(2)}) copy-start(bf16[1,896,1,256]{1,3,0,2:T(8,128)(2,1)} %get-tuple-element.6) | copy-start | bytes 1376260
  32.5 80.2 %collective-permute-start.5 = (bf16[1,896,1,256]{1,3,0,2:T(8,128)(2,1)}, bf16[1,896,1,256]{1,3,0,2:T(8,128)(2,1)S(1)}, u32[]{:S(2)}, u32[]{:S(2)}) collective-permute-start(bf16[1,896,1,256]{1,3,0,2:T(8,128)(2,1)} %get-tuple-element.14), channel_id=1, source_target_pairs={{0,6},{1,7},{2,8},{3,9},{4,10},{5,11},{6,12},{7,13},{8,14},{9,15},... | collective-permute-start | bytes 1376264 | tf_op jit(solution)/shard_map/ppermute | solution.py:33
  34.3 90.6 %collective-permute-start.6 = (bf16[1,896,1,256]{1,3,0,2:T(8,128)(2,1)}, bf16[1,896,1,256]{1,3,0,2:T(8,128)(2,1)S(1)}, u32[]{:S(2)}, u32[]{:S(2)}) collective-permute-start(bf16[1,896,1,256]{1,3,0,2:T(8,128)(2,1)} %get-tuple-element.13), channel_id=1, source_target_pairs={{0,7},{1,8},{2,9},{3,10},{4,11},{5,12},{6,13},{7,14},{8,15},{9,0},... | collective-permute-start | bytes 1376264 | tf_op jit(solution)/shard_map/ppermute | solution.py:33
  44.3 104.6 %collective-permute-start.7 = (bf16[1,896,1,256]{1,3,0,2:T(8,128)(2,1)}, bf16[1,896,1,256]{1,3,0,2:T(8,128)(2,1)S(1)}, u32[]{:S(2)}, u32[]{:S(2)}) collective-permute-start(bf16[1,896,1,256]{1,3,0,2:T(8,128)(2,1)} %get-tuple-element.12), channel_id=1, source_target_pairs={{0,8},{1,9},{2,10},{3,11},{4,12},{5,13},{6,14},{7,15},{8,0},{9,1},... | collective-permute-start | bytes 1376264 | tf_op jit(solution)/shard_map/ppermute | solution.py:33
  46.7 103.4 %collective-permute-start.8 = (bf16[1,896,1,256]{1,3,0,2:T(8,128)(2,1)}, bf16[1,896,1,256]{1,3,0,2:T(8,128)(2,1)S(1)}, u32[]{:S(2)}, u32[]{:S(2)}) collective-permute-start(bf16[1,896,1,256]{1,3,0,2:T(8,128)(2,1)} %get-tuple-element.11), channel_id=1, source_target_pairs={{0,9},{1,10},{2,11},{3,12},{4,13},{5,14},{6,15},{7,0},{8,1},{9,2},... | collective-permute-start | bytes 1376264 | tf_op jit(solution)/shard_map/ppermute | solution.py:33
  111.8 53.6 %collective-permute-start.9 = (bf16[1,896,1,256]{1,3,0,2:T(8,128)(2,1)}, bf16[1,896,1,256]{1,3,0,2:T(8,128)(2,1)S(1)}, u32[]{:S(2)}, u32[]{:S(2)}) collective-permute-start(bf16[1,896,1,256]{1,3,0,2:T(8,128)(2,1)} %get-tuple-element.10), channel_id=1, source_target_pairs={{0,10},{1,11},{2,12},{3,13},{4,14},{5,15},{6,0},{7,1},{8,2},{9,3},... | collective-permute-start | bytes 1376264 | tf_op jit(solution)/shard_map/ppermute | solution.py:33
  112.7 66.9 %collective-permute-start.10 = (bf16[1,896,1,256]{1,3,0,2:T(8,128)(2,1)S(1)}, bf16[1,896,1,256]{1,3,0,2:T(8,128)(2,1)S(1)}, u32[]{:S(2)}, u32[]{:S(2)}) collective-permute-start(bf16[1,896,1,256]{1,3,0,2:T(8,128)(2,1)S(1)} %copy-done.5), channel_id=1, source_target_pairs={{0,11},{1,12},{2,13},{3,14},{4,15},{5,0},{6,1},{7,2},{8,3},{9,4},{... | collective-permute-start | bytes 1376264 | tf_op jit(solution)/shard_map/ppermute | solution.py:33
  124.9 55.4 %collective-permute-start.11 = (bf16[1,896,1,256]{1,3,0,2:T(8,128)(2,1)S(1)}, bf16[1,896,1,256]{1,3,0,2:T(8,128)(2,1)S(1)}, u32[]{:S(2)}, u32[]{:S(2)}) collective-permute-start(bf16[1,896,1,256]{1,3,0,2:T(8,128)(2,1)S(1)} %copy-done.4), channel_id=1, source_target_pairs={{0,12},{1,13},{2,14},{3,15},{4,0},{5,1},{6,2},{7,3},{8,4},{9,5},{1... | collective-permute-start | bytes 1376264 | tf_op jit(solution)/shard_map/ppermute | solution.py:33
  148.9 32.3 %collective-permute-start.12 = (bf16[1,896,1,256]{1,3,0,2:T(8,128)(2,1)S(1)}, bf16[1,896,1,256]{1,3,0,2:T(8,128)(2,1)S(1)}, u32[]{:S(2)}, u32[]{:S(2)}) collective-permute-start(bf16[1,896,1,256]{1,3,0,2:T(8,128)(2,1)S(1)} %copy-done.3), channel_id=1, source_target_pairs={{0,13},{1,14},{2,15},{3,0},{4,1},{5,2},{6,3},{7,4},{8,5},{9,6},{10... | collective-permute-start | bytes 1376264 | tf_op jit(solution)/shard_map/ppermute | solution.py:33
  150.1 34.8 %collective-permute-start.13 = (bf16[1,896,1,256]{1,3,0,2:T(8,128)(2,1)S(1)}, bf16[1,896,1,256]{1,3,0,2:T(8,128)(2,1)S(1)}, u32[]{:S(2)}, u32[]{:S(2)}) collective-permute-start(bf16[1,896,1,256]{1,3,0,2:T(8,128)(2,1)S(1)} %copy-done.2), channel_id=1, source_target_pairs={{0,14},{1,15},{2,0},{3,1},{4,2},{5,3},{6,4},{7,5},{8,6},{9,7},{10,... | collective-permute-start | bytes 1376264 | tf_op jit(solution)/shard_map/ppermute | solution.py:33
  165.4 22.8 %collective-permute-start.14 = (bf16[1,896,1,256]{1,3,0,2:T(8,128)(2,1)S(1)}, bf16[1,896,1,256]{1,3,0,2:T(8,128)(2,1)S(1)}, u32[]{:S(2)}, u32[]{:S(2)}) collective-permute-start(bf16[1,896,1,256]{1,3,0,2:T(8,128)(2,1)S(1)} %get-tuple-element.5), channel_id=1, source_target_pairs={{0,15},{1,0},{2,1},{3,2},{4,3},{5,4},{6,5},{7,6},{8,7},{9,8},{10,9... | collective-permute-start | bytes 1376264 | tf_op jit(solution)/shard_map/ppermute | solution.py:33
  328.2 2.4 copy-start.1
  331.3 1.6 copy-start
